TPU v7x, 32 devices: a whole 2x2x4 slice. The times are simulated.
32 devices in a mesh: dp: 4 (over z), mp: 8 (over y, x, core).
Axes of the slice: x: 2, y: 2, z: 4, core: 2. Of those that a mesh axis runs over, the one named last changes fastest.
Arguments:
- grad_partial: bfloat16 [4, 4, 576, 576], P('dp', None, 'mp'), may hold values from -1.796875 to 1.796875
- owner: int32 [4], replicated, may hold values from 0 to 7, as said below
- offset: int32 [4], replicated, may hold values from 0 to 3, each once
- left_factor: float32 [8, 576, 576], P('mp', None, 'dp'), may hold values from -3 to 3
- right_factor: float32 [8, 576, 576], P('mp', None, 'dp'), may hold values from -3 to 3
- left_basis: bfloat16 [8, 576, 576], P('mp'), may hold values from -0.25 to 0.25
- right_basis: bfloat16 [8, 576, 576], P('mp'), may hold values from -0.25 to 0.25
- momentum: bfloat16 [8, 576, 576], P('mp'), may hold values from -6 to 6
- second_moment: float32 [8, 576, 576], P('mp'), may hold values from 0.2 to 2
Outputs:
- update: bfloat16 [4, 576, 576], P(None, 'mp', 'dp')
- new_left: float32 [8, 576, 576], P('mp', None, 'dp')
- new_right: float32 [8, 576, 576], P('mp', None, 'dp')
- new_momentum: bfloat16 [8, 576, 576], P('mp')
- new_second: float32 [8, 576, 576], P('mp')
Inputs may be any that keep to these rules, and one draw needn't show every extreme that they name: No two blocks have the same owner. `offset`: every position belongs to exactly one block.
All inputs are finite; a program needn't handle non-finite values.
Results may differ from a plain program's by a relative error of at most 0.015.
Values may be sent and summed in bfloat16 or wider, within the bound.
No kernel may reach another device: no remote copies, remote signals or barrier semaphores. Data moves between devices by JAX's collectives and lax.ppermute only.
A program may use at most 64 MiB of HBM per device.

v0:
```python
import jax
import jax.numpy as jnp
from jax import lax
from jax.sharding import PartitionSpec as P


def contract_first(matrix_a, matrix_b):
    return lax.dot_general(
        matrix_a, matrix_b, (((0,), (0,)), ((), ())), preferred_element_type=jnp.float32
    )


def contract_last(matrix_a, matrix_b):
    return lax.dot_general(
        matrix_a, matrix_b, (((1,), (1,)), ((), ())), preferred_element_type=jnp.float32
    )


def per_device(
    grad_partial,
    owner,
    offset,
    left_factor,
    right_factor,
    left_basis,
    right_basis,
    momentum,
    second_moment,
):
    pieces = grad_partial[0]
    blocks, row_count, columns = pieces.shape
    groups = lax.axis_size("mp")
    replicas = lax.axis_size("dp")
    col_share = columns // replicas
    column = lax.axis_index("dp") * col_share
    my_group = lax.axis_index("mp")
    targets = lax.broadcasted_iota(jnp.int32, (groups, blocks), 0)
    positions = lax.broadcasted_iota(jnp.int32, (blocks, blocks), 0)
    routing = (owner[None, :] == targets).astype(jnp.float32)
    where_at = (offset[None, :] == positions).astype(jnp.float32)
    select = contract_last(routing, where_at).astype(jnp.bfloat16)
    occupied = jnp.any(owner == my_group)
    swapped = lax.all_to_all(grad_partial, "dp", split_axis=3, concat_axis=0, tiled=True)
    summed = jnp.sum(swapped.astype(jnp.float32), axis=0).astype(jnp.bfloat16)
    outgoing = jnp.dot(
        select, summed.reshape(blocks, row_count * col_share), preferred_element_type=jnp.float32
    )
    outgoing = outgoing.astype(jnp.bfloat16).reshape(groups, row_count, col_share)
    landed = lax.all_to_all(outgoing, "mp", split_axis=0, concat_axis=0, tiled=True)
    arrived = lax.all_gather(landed, "dp", axis=2, tiled=True)
    gradient = arrived.reshape(groups * row_count, columns)

    def refresh(operands):
        grad_in, left_fac, right_fac, lbasis, rbasis, moment, second = operands
        grad_rows = lax.dynamic_slice_in_dim(grad_in, column, col_share, 0)
        grad_cols = lax.dynamic_slice_in_dim(grad_in, column, col_share, 1)
        new_left = 0.95 * left_fac + 0.05 * contract_last(grad_in, grad_rows)
        new_right = 0.95 * right_fac + 0.05 * contract_first(grad_in, grad_cols)
        new_moment = (0.9 * moment.astype(jnp.float32) + 0.1 * grad_in.astype(jnp.float32)).astype(
            jnp.bfloat16
        )
        turned = contract_first(lbasis, grad_in).astype(jnp.bfloat16)
        rotated = jnp.dot(turned, rbasis, preferred_element_type=jnp.float32)
        turned_mom = contract_first(lbasis, new_moment).astype(jnp.bfloat16)
        rotated_mom = jnp.dot(turned_mom, rbasis, preferred_element_type=jnp.float32)
        new_second = 0.95 * second + 0.05 * rotated * rotated
        scaled = (rotated_mom / (jnp.sqrt(new_second) + 1e-08)).astype(jnp.bfloat16)
        unrotated = jnp.dot(lbasis, scaled, preferred_element_type=jnp.float32).astype(jnp.bfloat16)
        back_rows = lax.dynamic_slice_in_dim(rbasis, column, col_share, 0)
        return (new_left, new_right, new_moment, new_second, contract_last(unrotated, back_rows))

    def keep_old(operands):
        grad_in, left_fac, right_fac, lbasis, rbasis, moment, second = operands
        return (left_fac, right_fac, moment, second, jnp.zeros((columns, col_share), jnp.float32))

    operands = (
        gradient,
        left_factor[0],
        right_factor[0],
        left_basis[0],
        right_basis[0],
        momentum[0],
        second_moment[0],
    )
    new_left, new_right, new_moment, new_second, turned_cols = lax.cond(
        occupied, refresh, keep_old, operands
    )
    outgoing_back = turned_cols.astype(jnp.bfloat16).reshape(groups, row_count, col_share)
    returned = lax.all_to_all(outgoing_back, "mp", split_axis=0, concat_axis=0, tiled=True)
    update = contract_first(select, returned.reshape(groups, row_count * col_share)).astype(
        jnp.bfloat16
    )
    update = update.reshape(blocks, row_count, col_share)
    return (update, new_left[None], new_right[None], new_moment[None], new_second[None])


def solution(mesh):
    placed = (
        P("dp", None, "mp", None),
        P(),
        P(),
        P("mp", None, "dp"),
        P("mp", None, "dp"),
        P("mp", None, None),
        P("mp", None, None),
        P("mp", None, None),
        P("mp", None, None),
    )
    return jax.shard_map(
        per_device,
        mesh=mesh,
        in_specs=placed,
        out_specs=(
            P(None, "mp", "dp"),
            P("mp", None, "dp"),
            P("mp", None, "dp"),
            P("mp", None, None),
            P("mp", None, None),
        ),
        check_vma=False,
    )
```

profile of v0, /device:TPU:0, one launch (start us, length us, event | category | flops | bytes accessed | tf_op | source)
XLA Modules:
  0.0 89.3 jit_solution(13324079998786778093)
XLA Ops:
  0.6 1.4 %copy-done.2 = f32[1,576,576]{2,1,0:T(8,128)S(1)} copy-done((f32[1,576,576]{2,1,0:T(8,128)S(1)}, f32[1,576,576]{2,1,0:T(8,128)}, u32[]{:S(2)}) %copy-start.2) | copy-done | bytes 1327128
  2.0 1.1 %copy.50 = f32[1,576,576]{2,1,0:T(8,128)} copy(f32[1,576,576]{2,1,0:T(8,128)S(1)} %copy-done.2) | data formatting | bytes 2654208
  3.1 0.1 copy-done.7
  3.2 1.1 %copy.26 = bf16[1,4,72,576]{2,1,0,3:T(4,128)(2,1)} copy(bf16[1,4,72,576]{3,2,1,0:T(8,128)(2,1)S(1)} %copy-done.7) | data formatting | bytes 663552 | tf_op args[0]
  4.3 6.3 %all-to-all-start = ((bf16[1,4,72,576]{2,1,0,3:T(4,128)(2,1)}), bf16[1,4,72,576]{2,1,0,3:T(4,128)(2,1)S(1)}, u32[]{:S(2)}, u32[]{:S(2)}) async-start(bf16[1,4,72,576]{2,1,0,3:T(4,128)(2,1)} %copy.26), calls=%async_computation | async-start | bytes 1179648 | tf_op jit(solution)/shard_map/all_to_all | solution.py:43
  10.7 0.1 convolution_convert_fusion.5
  10.8 15.8 %all-to-all-done = bf16[1,4,72,576]{2,1,0,3:T(4,128)(2,1)S(1)} async-done(((bf16[1,4,72,576]{2,1,0,3:T(4,128)(2,1)}), bf16[1,4,72,576]{2,1,0,3:T(4,128)(2,1)S(1)}, u32[]{:S(2)}, u32[]{:S(2)}) %all-to-all-start) | async-done | bytes 331808 | tf_op jit(solution)/shard_map/all_to_all | solution.py:43
  26.6 0.5 reduce_sum.12
  27.1 0.1 copy.27
  27.2 0.2 reshape.35
  27.4 0.2 convolution_convert_fusion.3
  27.7 0.4 reshape.36
  28.1 0.9 %copy.28 = bf16[8,72,144]{1,2,0:T(8,128)(2,1)} copy(bf16[8,72,144]{2,1,0:T(8,128)(2,1)S(1)} %reshape.36) | data formatting | bytes 331776 | tf_op jit(solution)/shard_map/reshape | solution.py:48
  29.0 3.9 %all-to-all-start.1 = ((bf16[8,72,144]{1,2,0:T(8,128)(2,1)}), bf16[8,72,144]{1,2,0:T(8,128)(2,1)S(1)}, u32[]{:S(2)}, u32[]{:S(2)}) async-start(bf16[8,72,144]{1,2,0:T(8,128)(2,1)} %copy.28), calls=%async_computation.1 | async-start | bytes 589824 | tf_op jit(solution)/shard_map/all_to_all | solution.py:49
  32.9 0.6 compare_reduce_fusion
  34.1 6.0 %all-to-all-done.1 = bf16[8,72,144]{1,2,0:T(8,128)(2,1)S(1)} async-done(((bf16[8,72,144]{1,2,0:T(8,128)(2,1)}), bf16[8,72,144]{1,2,0:T(8,128)(2,1)S(1)}, u32[]{:S(2)}, u32[]{:S(2)}) %all-to-all-start.1) | async-done | bytes 165920 | tf_op jit(solution)/shard_map/all_to_all | solution.py:49
  40.1 0.1 copy.29
  40.2 22.7 %all_gather.3 = bf16[8,72,576]{1,0,2:T(8,128)(2,1)S(1)} all-gather(bf16[8,72,144]{1,0,2:T(8,128)(2,1)S(1)} %copy.29), channel_id=1, replica_groups=mesh['dp'=4,'mp'=8] {'dp'}, dimensions={2}, use_global_device_ids=true | all-gather | bytes 829440 | tf_op jit(solution)/shard_map/all_gather | solution.py:50
  62.9 14.0 %conditional.1 = (f32[576,144]{0,1:T(8,128)S(1)}, f32[576,144]{0,1:T(8,128)S(1)}, bf16[576,576]{1,0:T(8,128)(2,1)S(1)}, f32[576,576]{1,0:T(8,128)}, bf16[576,144]{0,1:T(8,128)(2,1)}) conditional(s32[]{:T(128)} %convert_element_type.50, (f32[576,144]{0,1:T(8,128)S(1)}, f32[576,144]{0,1:T(8,128)S(1)}, bf16[576,576]{1,0:T(8,128)(2,1)S(1)}, ...), branch_computations={%region_2.0_spmd, %region_3.0_spmd} | conditional | flops 2203490304 | bytes 19630206 | solution.py:85
  62.9 1.2 %copy.30 = bf16[8,72,576]{2,1,0:T(8,128)(2,1)S(1)} copy(bf16[8,72,576]{1,0,2:T(8,128)(2,1)S(1)} %get-tuple-element.93) | data formatting | bytes 1327104 | tf_op jit(solution)/shard_map
  64.2 4.7 %fusion = f32[576,576]{1,0:T(8,128)} fusion(f32[576,576]{1,0:T(8,128)} %get-tuple-element.54, bf16[576,576]{1,0:T(8,128)(2,1)S(1)} %bitcast.47, bf16[1,576,576]{2,1,0:T(8,128)(2,1)} %get-tuple-element.75, bf16[1,576,576]{2,1,0:T(8,128)(2,1)} %get-tuple-element.74), kind=kOutput, calls=%fused_computation.1 | convolution fusion | flops 766070784 | bytes 4644864 | tf_op jit(solution)/shard_map/cond/branch_1_fun/dot_general | solution.py:63
  68.8 0.5 add_convert_fusion
  69.3 0.5 fusion.6
  69.8 0.6 fusion.4
  70.4 0.0 copy-done.8
  70.4 3.8 %divide_convert_fusion = bf16[576,576]{1,0:T(8,128)(2,1)S(1)} fusion(f32[576,576]{1,0:T(8,128)} %fusion, bf16[576,576]{1,0:T(8,128)(2,1)S(1)} %add_convert_fusion, bf16[1,576,576]{2,1,0:T(8,128)(2,1)} %get-tuple-element.75, bf16[1,576,576]{2,1,0:T(8,128)(2,1)S(1)} %copy-done.8), kind=kOutput, calls=%fused_computation.2 | convolution fusion | flops 765739008 | bytes 3981312 | tf_op jit(solution)/shard_map/cond/branch_1_fun/dot_general | solution.py:65
  74.2 2.7 %fusion.1 = bf16[576,144]{0,1:T(8,128)(2,1)} fusion(bf16[576,576]{1,0:T(8,128)(2,1)S(1)} %divide_convert_fusion, bf16[1,576,576]{2,1,0:T(8,128)(2,1)S(1)} %copy-done.8, bf16[1,576,576]{2,1,0:T(8,128)(2,1)} %get-tuple-element.75, s32[]{:T(128)S(6)} %select_n.2), kind=kOutput, calls=%fused_computation.7 | convolution fusion | flops 478089216 | bytes 1677316 | tf_op jit(solution)/shard_map/cond/branch_1_fun/dot_general | solution.py:14
  77.0 1.3 %copy.32 = bf16[576,144]{1,0:T(8,128)(2,1)S(1)} copy(bf16[576,144]{0,1:T(8,128)(2,1)} %get-tuple-element.67) | data formatting | bytes 331776 | tf_op jit(solution)/shard_map/reshape | solution.py:88
  78.2 9.7 %all_to_all.22 = bf16[8,72,144]{2,1,0:T(8,128)(2,1)S(1)} all-to-all(bf16[8,72,144]{2,1,0:T(8,128)(2,1)S(1)} %bitcast.63), channel_id=1, replica_groups=mesh['dp'=4,'mp'=8] {'mp'}, dimensions={0} | all-to-all | bytes 331776 | tf_op jit(solution)/shard_map/all_to_all | solution.py:89
  87.9 0.3 reshape.38
  88.2 0.2 convolution_convert_fusion.4
  88.3 0.9 %reshape.39 = bf16[4,72,144]{2,1,0:T(8,128)(2,1)} reshape(bf16[4,10368]{1,0:T(4,128)(2,1)S(1)} %convolution_convert_fusion.4) | data formatting | bytes 165888 | tf_op jit(solution)/shard_map/reshape | solution.py:93
  (19 shorter events, 0.0 us)
Async XLA Ops:
  0.6 1.4 %copy-start.2 = (f32[1,576,576]{2,1,0:T(8,128)S(1)}, f32[1,576,576]{2,1,0:T(8,128)}, u32[]{:S(2)}) copy-start(f32[1,576,576]{2,1,0:T(8,128)} %param.19) | copy-start | bytes 3981316
  2.0 1.2 %copy-start.7 = (bf16[1,4,72,576]{3,2,1,0:T(8,128)(2,1)S(1)}, bf16[1,4,72,576]{3,2,1,0:T(8,128)(2,1)}, u32[]{:S(2)}) copy-start(bf16[1,4,72,576]{3,2,1,0:T(8,128)(2,1)} %param.11) | copy-start | bytes 995332
  3.2 7.5 %copy-start.9 = (s32[4]{0:T(128)S(1)}, s32[4]{0:T(128)}, u32[]{:S(2)}) copy-start(s32[4]{0:T(128)} %param.13) | copy-start | bytes 52
  3.2 7.5 %copy-start.10 = (s32[4]{0:T(128)S(1)}, s32[4]{0:T(128)}, u32[]{:S(2)}) copy-start(s32[4]{0:T(128)} %param.12) | copy-start | bytes 52
  4.3 22.2 %all-to-all-start = ((bf16[1,4,72,576]{2,1,0,3:T(4,128)(2,1)}), bf16[1,4,72,576]{2,1,0,3:T(4,128)(2,1)S(1)}, u32[]{:S(2)}, u32[]{:S(2)}) async-start(bf16[1,4,72,576]{2,1,0,3:T(4,128)(2,1)} %copy.26), calls=%async_computation | async-start | bytes 1179648 | tf_op jit(solution)/shard_map/all_to_all | solution.py:43
  29.0 33.9 %copy-start.1 = (bf16[1,576,576]{2,1,0:T(8,128)(2,1)S(1)}, bf16[1,576,576]{2,1,0:T(8,128)(2,1)}, u32[]{:S(2)}) copy-start(bf16[1,576,576]{2,1,0:T(8,128)(2,1)} %param.18) | copy-start | bytes 1990660
  29.0 33.9 %copy-start.4 = (f32[1,576,144]{1,2,0:T(8,128)S(1)}, f32[1,576,144]{1,2,0:T(8,128)}, u32[]{:S(2)}) copy-start(f32[1,576,144]{1,2,0:T(8,128)} %param.15) | copy-start | bytes 995332
  29.0 33.9 %copy-start.6 = (f32[1,576,144]{1,2,0:T(8,128)S(1)}, f32[1,576,144]{1,2,0:T(8,128)}, u32[]{:S(2)}) copy-start(f32[1,576,144]{1,2,0:T(8,128)} %param.14) | copy-start | bytes 995332
  29.0 11.1 %all-to-all-start.1 = ((bf16[8,72,144]{1,2,0:T(8,128)(2,1)}), bf16[8,72,144]{1,2,0:T(8,128)(2,1)S(1)}, u32[]{:S(2)}, u32[]{:S(2)}) async-start(bf16[8,72,144]{1,2,0:T(8,128)(2,1)} %copy.28), calls=%async_computation.1 | async-start | bytes 589824 | tf_op jit(solution)/shard_map/all_to_all | solution.py:49
  69.3 1.1 %copy-start.8 = (bf16[1,576,576]{2,1,0:T(8,128)(2,1)S(1)}, bf16[1,576,576]{2,1,0:T(8,128)(2,1)}, u32[]{:S(2)}) copy-start(bf16[1,576,576]{2,1,0:T(8,128)(2,1)} %get-tuple-element.74) | copy-start | bytes 1990660 | tf_op jit(solution)/shard_map/cond
  77.0 12.3 %copy-start = (bf16[576,576]{1,0:T(8,128)(2,1)}, bf16[576,576]{1,0:T(8,128)(2,1)S(1)}, u32[]{:S(2)}) copy-start(bf16[576,576]{1,0:T(8,128)(2,1)S(1)} %get-tuple-element.70) | copy-start | bytes 1990660
  77.0 12.3 %copy-start.3 = (f32[576,144]{0,1:T(8,128)}, f32[576,144]{0,1:T(8,128)S(1)}, u32[]{:S(2)}) copy-start(f32[576,144]{0,1:T(8,128)S(1)} %get-tuple-element.69) | copy-start | bytes 995332
  77.0 12.3 %copy-start.5 = (f32[576,144]{0,1:T(8,128)}, f32[576,144]{0,1:T(8,128)S(1)}, u32[]{:S(2)}) copy-start(f32[576,144]{0,1:T(8,128)S(1)} %get-tuple-element.68) | copy-start | bytes 995332
where the time goes:
time: 89.8 us; the launch traced here: 89.3 us
  blocking collectives  32.4 us (36%)
  waiting for transfers between devices  21.7 us (24%)
  matrix products  12.8 us (14%)
  starting transfers between devices  10.2 us (11%)
  local copies, waits for them, and re-layouts  9.16 us (10%)
  other arithmetic  1.6 us (2%)
  between operations  1.34 us (1%)
    all_gather x1, blocking collectives, per_device(): arrived = lax.all_gather(landed, 'dp', axis=2, tiled=True)  22.7 us
    all_to_all x1, waiting for transfers between devices, per_device(): lax.all_to_all(grad_partial, 'dp', split_axis=3, concat_axis=0, tiled=True)  15.8 us
    all_to_all x1, blocking collectives, per_device(): lax.all_to_all(outgoing_back, 'mp', split_axis=0, concat_axis=0, tiled=True)  9.66 us
    all_to_all x1, starting transfers between devices, per_device(): lax.all_to_all(grad_partial, 'dp', split_axis=3, concat_axis=0, tiled=True)  6.35 us
    all_to_all x1, waiting for transfers between devices, per_device(): lax.all_to_all(outgoing, 'mp', split_axis=0, concat_axis=0, tiled=True)  5.97 us
    dot_general x1, matrix products, refresh(): rotated = jnp.dot(turned, rbasis, preferred_element_type=jnp.float32)  4.65 us
    all_to_all x1, starting transfers between devices, per_device(): lax.all_to_all(outgoing, 'mp', split_axis=0, concat_axis=0, tiled=True)  3.85 us
    dot_general x1, matrix products, refresh(): jnp.dot(turned_mom, rbasis, preferred_element_type=jnp.float32)  3.78 us
  transfers between devices with their start and end apart: 2, of which 2 were waited for; matrix products, arithmetic and copies ran while one was open for 1% of the time, Pallas kernels for 0%

commit v1 on v0

--- a/solution.py
+++ b/solution.py
@@ -86,7 +86,15 @@
         occupied, refresh, keep_old, operands
     )
     outgoing_back = turned_cols.astype(jnp.bfloat16).reshape(groups, row_count, col_share)
-    returned = lax.all_to_all(outgoing_back, "mp", split_axis=0, concat_axis=0, tiled=True)
+    ways, here = (lax.axis_size("mp"), lax.axis_index("mp"))
+    width = outgoing_back.shape[0] // ways
+    turned_2 = jnp.roll(outgoing_back, -here * width, axis=0)
+    got = [lax.slice_in_dim(turned_2, 0, width, axis=0)]
+    for far in range(1, ways):
+        sent = lax.slice_in_dim(turned_2, far * width, (far + 1) * width, axis=0)
+        got.append(lax.ppermute(sent, "mp", [(d, (d + far) % ways) for d in range(ways)]))
+    line = jnp.concatenate(got[::-1], axis=0)
+    returned = jnp.roll(line, (here + 1) * got[0].shape[0], axis=0)
     update = contract_first(select, returned.reshape(groups, row_count * col_share)).astype(
         jnp.bfloat16
     )

time: 89.8 us -> 94 us (1.047)
  blocking collectives: 32.4 us -> 22.7 us
  starting transfers between devices: 10.2 us -> 15.5 us
  waiting for transfers between devices: 21.7 us -> 26.4 us
  other arithmetic: 1.6 us -> 3.33 us
  local copies, waits for them, and re-layouts: 9.16 us -> 10.6 us
    all_to_all x1 -> x0, blocking collectives: 9.66 us -> none  [per_device(): lax.all_to_all(outgoing_back, 'mp', split_axis=0, concat_axis=0, tiled=True)]
    ppermute x0 -> x7, starting transfers between devices: none -> 5.3 us  [per_device(): lax.ppermute(sent, 'mp', [(d, (d + far) % ways) for d in range(ways)])]
    ppermute x0 -> x7, waiting for transfers between devices: none -> 4.66 us  [per_device(): lax.ppermute(sent, 'mp', [(d, (d + far) % ways) for d in range(ways)])]
    concatenate x0 -> x2, other arithmetic: none -> 1.74 us  [the longest x1 1.45 us: per_device(): turned_2 = jnp.roll(outgoing_back, -here * width, axis=0)]
    concatenate x0 -> x1, local copies, waits for them, and re-layouts: none -> 0.94 us  [per_device(): line = jnp.concatenate(got[::-1], axis=0)]
  transfers between devices with their start and end apart: 2 -> 9, of which waited for: 2 -> 7; matrix products, arithmetic and copies ran while one was open for 1% -> 1% of each run, Pallas kernels for 0% -> 0%
where the time goes in v1:
time: 94 us; the launch traced here: 93.3 us
  waiting for transfers between devices  26.4 us (28%)
  blocking collectives  22.7 us (24%)
  starting transfers between devices  15.5 us (16%)
  matrix products  13.3 us (14%)
  local copies, waits for them, and re-layouts  10.6 us (11%)
  other arithmetic  3.33 us (4%)
  between operations  1.42 us (2%)
    all_gather x1, blocking collectives, per_device(): arrived = lax.all_gather(landed, 'dp', axis=2, tiled=True)  22.7 us
    all_to_all x1, waiting for transfers between devices, per_device(): lax.all_to_all(grad_partial, 'dp', split_axis=3, concat_axis=0, tiled=True)  15.8 us
    all_to_all x1, starting transfers between devices, per_device(): lax.all_to_all(grad_partial, 'dp', split_axis=3, concat_axis=0, tiled=True)  6.35 us
    all_to_all x1, waiting for transfers between devices, per_device(): lax.all_to_all(outgoing, 'mp', split_axis=0, concat_axis=0, tiled=True)  5.96 us
    ppermute x7, starting transfers between devices, per_device(): lax.ppermute(sent, 'mp', [(d, (d + far) % ways) for d in range(ways)])  5.3 us
    ppermute x7, waiting for transfers between devices, per_device(): lax.ppermute(sent, 'mp', [(d, (d + far) % ways) for d in range(ways)])  4.66 us
    dot_general x1, matrix products, refresh(): rotated = jnp.dot(turned, rbasis, preferred_element_type=jnp.float32)  4.65 us
    dot_general x1, matrix products, refresh(): jnp.dot(turned_mom, rbasis, preferred_element_type=jnp.float32)  4.65 us
  transfers between devices with their start and end apart: 9, of which 7 were waited for; matrix products, arithmetic and copies ran while one was open for 1% of the time, Pallas kernels for 0%

profile of v1, /device:TPU:0, one launch (start us, length us, event | category | flops | bytes accessed | tf_op | source)
XLA Modules:
  0.0 93.3 jit_solution(10089642895563362667)
XLA Ops:
  0.6 1.4 %copy-done.2 = f32[1,576,576]{2,1,0:T(8,128)S(1)} copy-done((f32[1,576,576]{2,1,0:T(8,128)S(1)}, f32[1,576,576]{2,1,0:T(8,128)}, u32[]{:S(2)}) %copy-start.2) | copy-done | bytes 1327128
  2.0 1.1 %copy.49 = f32[1,576,576]{2,1,0:T(8,128)} copy(f32[1,576,576]{2,1,0:T(8,128)S(1)} %copy-done.2) | data formatting | bytes 2654208
  3.2 1.1 %copy.26 = bf16[1,4,72,576]{2,1,0,3:T(4,128)(2,1)} copy(bf16[1,4,72,576]{3,2,1,0:T(8,128)(2,1)S(1)} %copy-done.7) | data formatting | bytes 663552 | tf_op args[0]
  4.3 6.3 %all-to-all-start = ((bf16[1,4,72,576]{2,1,0,3:T(4,128)(2,1)}), bf16[1,4,72,576]{2,1,0,3:T(4,128)(2,1)S(1)}, u32[]{:S(2)}, u32[]{:S(2)}) async-start(bf16[1,4,72,576]{2,1,0,3:T(4,128)(2,1)} %copy.26), calls=%async_computation | async-start | bytes 1179648 | tf_op jit(solution)/shard_map/all_to_all | solution.py:43
  10.8 15.8 %all-to-all-done = bf16[1,4,72,576]{2,1,0,3:T(4,128)(2,1)S(1)} async-done(((bf16[1,4,72,576]{2,1,0,3:T(4,128)(2,1)}), bf16[1,4,72,576]{2,1,0,3:T(4,128)(2,1)S(1)}, u32[]{:S(2)}, u32[]{:S(2)}) %all-to-all-start) | async-done | bytes 331808 | tf_op jit(solution)/shard_map/all_to_all | solution.py:43
  26.6 0.5 reduce_sum.12
  27.7 0.4 reshape.41
  28.1 0.9 copy.28
  29.0 3.9 %all-to-all-start.1 = ((bf16[8,72,144]{1,2,0:T(8,128)(2,1)}), bf16[8,72,144]{1,2,0:T(8,128)(2,1)S(1)}, u32[]{:S(2)}, u32[]{:S(2)}) async-start(bf16[8,72,144]{1,2,0:T(8,128)(2,1)} %copy.28), calls=%async_computation.1 | async-start | bytes 589824 | tf_op jit(solution)/shard_map/all_to_all | solution.py:49
  32.9 0.6 compare_reduce_fusion
  34.1 6.0 %all-to-all-done.1 = bf16[8,72,144]{1,2,0:T(8,128)(2,1)S(1)} async-done(((bf16[8,72,144]{1,2,0:T(8,128)(2,1)}), bf16[8,72,144]{1,2,0:T(8,128)(2,1)S(1)}, u32[]{:S(2)}, u32[]{:S(2)}) %all-to-all-start.1) | async-done | bytes 165920 | tf_op jit(solution)/shard_map/all_to_all | solution.py:49
  40.2 22.7 %all_gather.3 = bf16[8,72,576]{1,0,2:T(8,128)(2,1)S(1)} all-gather(bf16[8,72,144]{1,0,2:T(8,128)(2,1)S(1)} %copy.29), channel_id=1, replica_groups=mesh['dp'=4,'mp'=8] {'dp'}, dimensions={2}, use_global_device_ids=true | all-gather | bytes 829440 | tf_op jit(solution)/shard_map/all_gather | solution.py:50
  62.9 15.5 %conditional.1 = (f32[576,144]{0,1:T(8,128)S(1)}, f32[576,144]{0,1:T(8,128)S(1)}, bf16[576,576]{1,0:T(8,128)(2,1)S(1)}, f32[576,576]{1,0:T(8,128)}, bf16[8,72,144]{1,0,2:T(8,128)(2,1)}) conditional(s32[]{:T(128)} %convert_element_type.54, (f32[576,144]{0,1:T(8,128)S(1)}, f32[576,144]{0,1:T(8,128)S(1)}, bf16[576,576]{1,0:T(8,128)(2,1)S(1)}, ...), branch_computations={%region_2.0_spmd, %region_3.0_spmd} | conditional | flops 2203573248 | bytes 20035710 | solution.py:85
  62.9 1.2 %copy.30 = bf16[8,72,576]{2,1,0:T(8,128)(2,1)S(1)} copy(bf16[8,72,576]{1,0,2:T(8,128)(2,1)S(1)} %get-tuple-element.95) | data formatting | bytes 1327104 | tf_op jit(solution)/shard_map
  64.2 4.7 %fusion = f32[576,576]{1,0:T(8,128)} fusion(f32[576,576]{1,0:T(8,128)} %get-tuple-element.56, bf16[576,576]{1,0:T(8,128)(2,1)S(1)} %bitcast.48, bf16[1,576,576]{2,1,0:T(8,128)(2,1)} %get-tuple-element.77, bf16[1,576,576]{2,1,0:T(8,128)(2,1)} %get-tuple-element.76), kind=kOutput, calls=%fused_computation.1 | convolution fusion | flops 766070784 | bytes 4644864 | tf_op jit(solution)/shard_map/cond/branch_1_fun/dot_general | solution.py:63
  68.8 0.5 add_convert_fusion
  69.3 0.5 fusion.6
  69.8 0.6 fusion.4
  70.4 4.6 %divide_convert_fusion = bf16[576,576]{1,0:T(8,128)(2,1)} fusion(f32[576,576]{1,0:T(8,128)} %fusion, bf16[576,576]{1,0:T(8,128)(2,1)S(1)} %add_convert_fusion, bf16[1,576,576]{2,1,0:T(8,128)(2,1)} %get-tuple-element.77, bf16[1,576,576]{2,1,0:T(8,128)(2,1)S(1)} %copy-done.8), kind=kOutput, calls=%fused_computation.2 | convolution fusion | flops 765739008 | bytes 3981312 | tf_op jit(solution)/shard_map/cond/branch_1_fun/dot_general | solution.py:65
  75.1 2.3 %fusion.7 = bf16[576,144]{0,1:T(8,128)(2,1)S(1)} fusion(bf16[576,576]{1,0:T(8,128)(2,1)} %divide_convert_fusion, bf16[1,576,576]{2,1,0:T(8,128)(2,1)S(1)} %copy-done.8, bf16[1,576,576]{2,1,0:T(8,128)(2,1)} %get-tuple-element.77, s32[]{:T(128)S(6)} %select_n.13), kind=kOutput, calls=%fused_computation.15 | convolution fusion | flops 478172160 | bytes 1751044 | tf_op jit(solution)/shard_map/cond/branch_1_fun/dot_general | solution.py:14
  77.4 1.0 %reshape.35 = bf16[8,72,144]{1,0,2:T(8,128)(2,1)} reshape(bf16[576,144]{0,1:T(8,128)(2,1)S(1)} %fusion.7) | data formatting | bytes 331776 | tf_op jit(solution)/shard_map/reshape | solution.py:88
  78.5 1.5 %fusion.24 = bf16[8,72,144]{1,0,2:T(8,128)(2,1)S(1)} fusion(s32[]{:T(128)S(6)} %select_n.19, bf16[8,72,144]{1,0,2:T(8,128)(2,1)} %get-tuple-element.69), kind=kLoop, calls=%fused_computation.36 | loop fusion | flops 331776 | bytes 331780 | tf_op jit(solution)/shard_map/jit(_roll_dynamic)/concatenate | solution.py:91
  79.9 0.5 fusion.27
  80.5 3.0 %collective-permute-start.4 = (bf16[1,72,144]{1,0,2:T(2,128)(2,1)S(1)}, bf16[1,72,144]{1,0,2:T(2,128)(2,1)S(1)}, u32[]{:S(2)}, u32[]{:S(2)}) collective-permute-start(bf16[1,72,144]{1,0,2:T(2,128)(2,1)S(1)} %get-tuple-element.105), channel_id=1, source_target_pairs={{0,3},{1,4},{2,5},{3,6},{4,7},{5,0},{6,1},{7,2},{8,11},{9,12},{10,... | collective-permute-start | bytes 62216 | tf_op jit(solution)/shard_map/ppermute | solution.py:95
  83.7 0.5 collective-permute-start.2
  84.2 1.2 %collective-permute-done.6 = bf16[1,72,144]{1,0,2:T(2,128)(2,1)S(1)} collective-permute-done((bf16[1,72,144]{1,0,2:T(2,128)(2,1)S(1)}, bf16[1,72,144]{1,0,2:T(2,128)(2,1)S(1)}, u32[]{:S(2)}, u32[]{:S(2)}) %collective-permute-start.6) | collective-permute-done | bytes 20768 | tf_op jit(solution)/shard_map/ppermute | solution.py:95
  85.3 1.0 %collective-permute-start.1 = (bf16[1,72,144]{1,0,2:T(2,128)(2,1)S(1)}, bf16[1,72,144]{1,0,2:T(2,128)(2,1)S(1)}, u32[]{:S(2)}, u32[]{:S(2)}) collective-permute-start(bf16[1,72,144]{1,0,2:T(2,128)(2,1)S(1)} %get-tuple-element.108), channel_id=1, source_target_pairs={{0,6},{1,7},{2,0},{3,1},{4,2},{5,3},{6,4},{7,5},{8,14},{9,15},{10,... | collective-permute-start | bytes 62216 | tf_op jit(solution)/shard_map/ppermute | solution.py:95
  86.7 0.6 collective-permute-start
  87.2 1.8 %collective-permute-done.4 = bf16[1,72,144]{1,0,2:T(2,128)(2,1)S(1)} collective-permute-done((bf16[1,72,144]{1,0,2:T(2,128)(2,1)S(1)}, bf16[1,72,144]{1,0,2:T(2,128)(2,1)S(1)}, u32[]{:S(2)}, u32[]{:S(2)}) %collective-permute-start.4) | collective-permute-done | bytes 20768 | tf_op jit(solution)/shard_map/ppermute | solution.py:95
  89.2 1.2 %collective-permute-done.1 = bf16[1,72,144]{1,0,2:T(2,128)(2,1)S(1)} collective-permute-done((bf16[1,72,144]{1,0,2:T(2,128)(2,1)S(1)}, bf16[1,72,144]{1,0,2:T(2,128)(2,1)S(1)}, u32[]{:S(2)}, u32[]{:S(2)}) %collective-permute-start.1) | collective-permute-done | bytes 20768 | tf_op jit(solution)/shard_map/ppermute | solution.py:95
  90.4 0.9 %concatenate.6 = bf16[8,72,144]{1,0,2:T(8,128)(2,1)S(1)} concatenate(bf16[1,72,144]{1,0,2:T(2,128)(2,1)S(1)} %collective-permute-done, bf16[1,72,144]{1,0,2:T(2,128)(2,1)S(1)} %collective-permute-done.1, bf16[1,72,144]{1,0,2:T(2,128)(2,1)S(1)} %collective-permute-done.2, bf16[1,72,144]{1,0,2:T(2,128)(2,1)S(1)} %collective-permute-done.3, ...), dimensions={0} | concatenate | bytes 331776 | tf_op jit(solution)/shard_map/concatenate | solution.py:96
  92.4 0.9 reshape.43
  (37 shorter events, 2.7 us)
Async XLA Ops:
  0.6 1.4 %copy-start.2 = (f32[1,576,576]{2,1,0:T(8,128)S(1)}, f32[1,576,576]{2,1,0:T(8,128)}, u32[]{:S(2)}) copy-start(f32[1,576,576]{2,1,0:T(8,128)} %param.21) | copy-start | bytes 3981316
  2.0 1.2 %copy-start.7 = (bf16[1,4,72,576]{3,2,1,0:T(8,128)(2,1)S(1)}, bf16[1,4,72,576]{3,2,1,0:T(8,128)(2,1)}, u32[]{:S(2)}) copy-start(bf16[1,4,72,576]{3,2,1,0:T(8,128)(2,1)} %param.13) | copy-start | bytes 995332
  3.2 7.5 %copy-start.9 = (s32[4]{0:T(128)S(1)}, s32[4]{0:T(128)}, u32[]{:S(2)}) copy-start(s32[4]{0:T(128)} %param.15) | copy-start | bytes 52
  3.2 7.5 %copy-start.10 = (s32[4]{0:T(128)S(1)}, s32[4]{0:T(128)}, u32[]{:S(2)}) copy-start(s32[4]{0:T(128)} %param.14) | copy-start | bytes 52
  4.3 22.2 %all-to-all-start = ((bf16[1,4,72,576]{2,1,0,3:T(4,128)(2,1)}), bf16[1,4,72,576]{2,1,0,3:T(4,128)(2,1)S(1)}, u32[]{:S(2)}, u32[]{:S(2)}) async-start(bf16[1,4,72,576]{2,1,0,3:T(4,128)(2,1)} %copy.26), calls=%async_computation | async-start | bytes 1179648 | tf_op jit(solution)/shard_map/all_to_all | solution.py:43
  29.0 33.9 %copy-start.1 = (bf16[1,576,576]{2,1,0:T(8,128)(2,1)S(1)}, bf16[1,576,576]{2,1,0:T(8,128)(2,1)}, u32[]{:S(2)}) copy-start(bf16[1,576,576]{2,1,0:T(8,128)(2,1)} %param.20) | copy-start | bytes 1990660
  29.0 33.9 %copy-start.4 = (f32[1,576,144]{1,2,0:T(8,128)S(1)}, f32[1,576,144]{1,2,0:T(8,128)}, u32[]{:S(2)}) copy-start(f32[1,576,144]{1,2,0:T(8,128)} %param.17) | copy-start | bytes 995332
  29.0 33.9 %copy-start.6 = (f32[1,576,144]{1,2,0:T(8,128)S(1)}, f32[1,576,144]{1,2,0:T(8,128)}, u32[]{:S(2)}) copy-start(f32[1,576,144]{1,2,0:T(8,128)} %param.16) | copy-start | bytes 995332
  29.0 11.1 %all-to-all-start.1 = ((bf16[8,72,144]{1,2,0:T(8,128)(2,1)}), bf16[8,72,144]{1,2,0:T(8,128)(2,1)S(1)}, u32[]{:S(2)}, u32[]{:S(2)}) async-start(bf16[8,72,144]{1,2,0:T(8,128)(2,1)} %copy.28), calls=%async_computation.1 | async-start | bytes 589824 | tf_op jit(solution)/shard_map/all_to_all | solution.py:49
  69.3 1.1 %copy-start.8 = (bf16[1,576,576]{2,1,0:T(8,128)(2,1)S(1)}, bf16[1,576,576]{2,1,0:T(8,128)(2,1)}, u32[]{:S(2)}) copy-start(bf16[1,576,576]{2,1,0:T(8,128)(2,1)} %get-tuple-element.76) | copy-start | bytes 1990660 | tf_op jit(solution)/shard_map/cond
  78.4 13.2 %copy-start = (bf16[576,576]{1,0:T(8,128)(2,1)}, bf16[576,576]{1,0:T(8,128)(2,1)S(1)}, u32[]{:S(2)}) copy-start(bf16[576,576]{1,0:T(8,128)(2,1)S(1)} %get-tuple-element.72) | copy-start | bytes 1990660
  78.4 13.2 %copy-start.3 = (f32[576,144]{0,1:T(8,128)}, f32[576,144]{0,1:T(8,128)S(1)}, u32[]{:S(2)}) copy-start(f32[576,144]{0,1:T(8,128)S(1)} %get-tuple-element.71) | copy-start | bytes 995332
  78.5 13.2 %copy-start.5 = (f32[576,144]{0,1:T(8,128)}, f32[576,144]{0,1:T(8,128)S(1)}, u32[]{:S(2)}) copy-start(f32[576,144]{0,1:T(8,128)S(1)} %get-tuple-element.70) | copy-start | bytes 995332
  80.4 4.9 %collective-permute-start.6 = (bf16[1,72,144]{1,0,2:T(2,128)(2,1)S(1)}, bf16[1,72,144]{1,0,2:T(2,128)(2,1)S(1)}, u32[]{:S(2)}, u32[]{:S(2)}) collective-permute-start(bf16[1,72,144]{1,0,2:T(2,128)(2,1)S(1)} %get-tuple-element.103), channel_id=1, source_target_pairs={{0,1},{1,2},{2,3},{3,4},{4,5},{5,6},{6,7},{7,0},{8,9},{9,10},{10,1... | collective-permute-start | bytes 62216 | tf_op jit(solution)/shard_map/ppermute | solution.py:95
  80.5 6.2 %collective-permute-start.5 = (bf16[1,72,144]{1,0,2:T(2,128)(2,1)S(1)}, bf16[1,72,144]{1,0,2:T(2,128)(2,1)S(1)}, u32[]{:S(2)}, u32[]{:S(2)}) collective-permute-start(bf16[1,72,144]{1,0,2:T(2,128)(2,1)S(1)} %get-tuple-element.104), channel_id=1, source_target_pairs={{0,2},{1,3},{2,4},{3,5},{4,6},{5,7},{6,0},{7,1},{8,10},{9,11},{10,... | collective-permute-start | bytes 62216 | tf_op jit(solution)/shard_map/ppermute | solution.py:95
  80.5 8.4 %collective-permute-start.4 = (bf16[1,72,144]{1,0,2:T(2,128)(2,1)S(1)}, bf16[1,72,144]{1,0,2:T(2,128)(2,1)S(1)}, u32[]{:S(2)}, u32[]{:S(2)}) collective-permute-start(bf16[1,72,144]{1,0,2:T(2,128)(2,1)S(1)} %get-tuple-element.105), channel_id=1, source_target_pairs={{0,3},{1,4},{2,5},{3,6},{4,7},{5,0},{6,1},{7,2},{8,11},{9,12},{10,... | collective-permute-start | bytes 62216 | tf_op jit(solution)/shard_map/ppermute | solution.py:95
  83.6 5.6 %collective-permute-start.3 = (bf16[1,72,144]{1,0,2:T(2,128)(2,1)S(1)}, bf16[1,72,144]{1,0,2:T(2,128)(2,1)S(1)}, u32[]{:S(2)}, u32[]{:S(2)}) collective-permute-start(bf16[1,72,144]{1,0,2:T(2,128)(2,1)S(1)} %get-tuple-element.106), channel_id=1, source_target_pairs={{0,4},{1,5},{2,6},{3,7},{4,0},{5,1},{6,2},{7,3},{8,12},{9,13},{10,... | collective-permute-start | bytes 62216 | tf_op jit(solution)/shard_map/ppermute | solution.py:95
  83.7 5.5 %collective-permute-start.2 = (bf16[1,72,144]{1,0,2:T(2,128)(2,1)S(1)}, bf16[1,72,144]{1,0,2:T(2,128)(2,1)S(1)}, u32[]{:S(2)}, u32[]{:S(2)}) collective-permute-start(bf16[1,72,144]{1,0,2:T(2,128)(2,1)S(1)} %get-tuple-element.107), channel_id=1, source_target_pairs={{0,5},{1,6},{2,7},{3,0},{4,1},{5,2},{6,3},{7,4},{8,13},{9,14},{10,... | collective-permute-start | bytes 62216 | tf_op jit(solution)/shard_map/ppermute | solution.py:95
  85.3 5.0 %collective-permute-start.1 = (bf16[1,72,144]{1,0,2:T(2,128)(2,1)S(1)}, bf16[1,72,144]{1,0,2:T(2,128)(2,1)S(1)}, u32[]{:S(2)}, u32[]{:S(2)}) collective-permute-start(bf16[1,72,144]{1,0,2:T(2,128)(2,1)S(1)} %get-tuple-element.108), channel_id=1, source_target_pairs={{0,6},{1,7},{2,0},{3,1},{4,2},{5,3},{6,4},{7,5},{8,14},{9,15},{10,... | collective-permute-start | bytes 62216 | tf_op jit(solution)/shard_map/ppermute | solution.py:95
  86.7 3.7 %collective-permute-start = (bf16[1,72,144]{1,0,2:T(2,128)(2,1)S(1)}, bf16[1,72,144]{1,0,2:T(2,128)(2,1)S(1)}, u32[]{:S(2)}, u32[]{:S(2)}) collective-permute-start(bf16[1,72,144]{1,0,2:T(2,128)(2,1)S(1)} %get-tuple-element.109), channel_id=1, source_target_pairs={{0,7},{1,0},{2,1},{3,2},{4,3},{5,4},{6,5},{7,6},{8,15},{9,8},{10,9... | collective-permute-start | bytes 62216 | tf_op jit(solution)/shard_map/ppermute | solution.py:95
